TPU v7x, 32 devices: a whole 2x2x4 slice. The times are simulated.
32 devices in a mesh: grp: 4 (over y, core), dev: 8 (over z, x).
Axes of the slice: x: 2, y: 2, z: 4, core: 2. Of those that a mesh axis runs over, the one named last changes fastest.
Arguments:
- densities: bfloat16 [32, 200, 200], P(('grp', 'dev')), may hold values from -0.4375 to 0.4375
- core_hamiltonian: bfloat16 [32, 200, 200], P(('grp', 'dev')), may hold values from -0.21875 to 0.21875
- embedding: bfloat16 [32, 200, 200], P(('grp', 'dev')), may hold values from -0.21875 to 0.21875
- fit_factors: bfloat16 [192, 200, 200], P('dev'), may hold values from -0.059814453 to 0.059814453
- orthogonalizers: bfloat16 [32, 200, 200], P(('grp', 'dev'))
- pairs: int32 [384, 2], replicated, may hold values from 0 to 31, as said below
- assignment: int32 [384], replicated, may hold values from 0 to 7, as said below
- owner_map: int32 [32], replicated, may hold values from 0 to 31, as said below
Outputs:
- slot_energies: float32 [768], P(('grp', 'dev'))
- total: float32 [], replicated
Inputs may be any that keep to these rules, and one draw needn't show every extreme that they name: `pairs`: dimer k belongs to group g = k // 96; its first fragment lies in block g, the fragments g * 8 to (g + 1) * 8 - 1, and its second fragment, different from the first, lies in block g or block g + 1 (only block g for the last group). `assignment`: no device receives more than 24 dimers of its group, and in every group some device receives exactly 24. `owner_map`: A permutation of the fragments that maps each block of 8 fragments onto the rows of the same block.
All inputs are finite; a program needn't handle non-finite values.
Results may differ from a plain program's by a relative error of at most 0.0003.
Values may be sent and summed in bfloat16 or wider, within the bound.
A program may use at most 128 MiB of HBM per device.

v0:
```python
import jax
import jax.numpy as jnp
from jax import lax
from jax.sharding import PartitionSpec as P

DIM_DEV = 12
SLOTS = 24


HALF_WIDTH = 4.0


def from_behind(block, axis, distance):
    devices = range(lax.axis_size(axis))
    route = [(i - distance, i) for i in devices if i - distance in devices]
    return lax.ppermute(block, axis, route)


def product(left, right):
    return jnp.dot(left, right, preferred_element_type=jnp.float32)


def dimer_energy(fock_i, fock_j, dens_i, dens_j, ortho_i, ortho_j):
    coupling = (0.5 * (product(fock_i, dens_j) + product(dens_i, fock_j))).astype(jnp.bfloat16)
    upper_left = product(fock_i, ortho_i).astype(jnp.bfloat16)
    upper_right = product(coupling, ortho_j).astype(jnp.bfloat16)
    lower_left = product(coupling.T, ortho_i).astype(jnp.bfloat16)
    lower_right = product(fock_j, ortho_j).astype(jnp.bfloat16)
    top_rows = jnp.concatenate(
        [product(ortho_i.T, upper_left), product(ortho_i.T, upper_right)], axis=1
    )
    bottom_rows = jnp.concatenate(
        [product(ortho_j.T, lower_left), product(ortho_j.T, lower_right)], axis=1
    )
    ortho_fock = jnp.concatenate([top_rows, bottom_rows], axis=0)
    size_two = ortho_fock.shape[0]
    half_basis = fock_i.shape[0]
    start = (0.5 * jnp.eye(size_two, dtype=jnp.float32) - ortho_fock / (2.0 * HALF_WIDTH)).astype(
        jnp.bfloat16
    )
    square = product(start, start).astype(jnp.bfloat16)
    cube = product(square, start)
    purified = (3.0 * square.astype(jnp.float32) - 2.0 * cube).astype(jnp.bfloat16)
    left_part = jnp.concatenate(
        [product(ortho_i, purified[:half_basis]), product(ortho_j, purified[half_basis:])], axis=0
    ).astype(jnp.bfloat16)
    new_density = jnp.concatenate(
        [
            product(left_part[:, :half_basis], ortho_i.T),
            product(left_part[:, half_basis:], ortho_j.T),
        ],
        axis=1,
    )
    fock_top = jnp.concatenate([fock_i, coupling], axis=1)
    fock_bottom = jnp.concatenate([coupling.T, fock_j], axis=1)
    dimer_fock = jnp.concatenate([fock_top, fock_bottom], axis=0).astype(jnp.float32)
    monomer_i = jnp.sum(dens_i.astype(jnp.float32) * fock_i.astype(jnp.float32))
    monomer_j = jnp.sum(dens_j.astype(jnp.float32) * fock_j.astype(jnp.float32))
    return jnp.sum(new_density * dimer_fock) - monomer_i - monomer_j


def on_device(
    densities,
    core_hamiltonian,
    embedding,
    fit_factors,
    orthogonalizers,
    pairs,
    assignment,
    owner_map,
):
    members = lax.axis_size("dev")
    group_index = lax.axis_index("grp")
    member_index = lax.axis_index("dev")
    basis_size = densities.shape[1]
    aux_count = fit_factors.shape[0]
    flat_fit = fit_factors.reshape(aux_count, basis_size * basis_size)
    gathered = lax.all_gather(densities, "dev", axis=0, tiled=True)
    flat_dens = gathered.reshape(members, basis_size * basis_size)
    coeffs = lax.dot_general(
        flat_dens, flat_fit, (((1,), (1,)), ((), ())), preferred_element_type=jnp.float32
    ).astype(jnp.bfloat16)
    coulomb = lax.psum_scatter(
        jnp.dot(coeffs, flat_fit, preferred_element_type=jnp.float32)
        .reshape(densities.shape[0] * lax.axis_size("dev"), basis_size, basis_size)
        .astype(jnp.bfloat16),
        "dev",
        scatter_dimension=0,
        tiled=True,
    ).astype(jnp.float32)
    fock_rows = (
        core_hamiltonian.astype(jnp.float32) + embedding.astype(jnp.float32) + coulomb
    ).astype(jnp.bfloat16)
    local_pair = jnp.stack([fock_rows, orthogonalizers], axis=1)
    monomer = jnp.stack([fock_rows, densities, orthogonalizers], axis=1)
    following = from_behind(monomer, "grp", -1)
    own_pair, next_pool = (
        lax.all_gather(local_pair, "dev", axis=0, tiled=True),
        lax.all_gather(following, "dev", axis=0, tiled=True),
    )
    dim_group = DIM_DEV * members
    group_pairs = lax.dynamic_slice_in_dim(pairs, group_index * dim_group, dim_group, 0)
    group_assign = lax.dynamic_slice_in_dim(assignment, group_index * dim_group, dim_group, 0)
    is_mine = group_assign == member_index
    mine_count = is_mine.astype(jnp.int32)
    before = jnp.cumsum(mine_count) - mine_count
    select = is_mine[None, :] & (before[None, :] == jnp.arange(SLOTS, dtype=jnp.int32)[:, None])
    list_positions = jnp.arange(dim_group, dtype=jnp.int32)

    def energy_of(listed):
        pair_ids = group_pairs[listed]
        first_row = owner_map[pair_ids[0]] - group_index * members
        second_row = owner_map[pair_ids[1]] - group_index * members
        in_next = second_row >= members
        pool_row = jnp.where(in_next, second_row - members, second_row)
        first_pair = own_pair[first_row]
        own_second = own_pair[pool_row]
        next_second = next_pool[pool_row]
        second_fock = jnp.where(in_next, next_second[0], own_second[0])
        second_dens = jnp.where(in_next, next_second[1], gathered[pool_row])
        second_ortho = jnp.where(in_next, next_second[2], own_second[1])
        return dimer_energy(
            first_pair[0],
            second_fock,
            gathered[first_row],
            second_dens,
            first_pair[1],
            second_ortho,
        )

    listed = member_index * DIM_DEV + jnp.arange(DIM_DEV, dtype=jnp.int32)
    values = lax.map(energy_of, listed)
    spread = jnp.sum(
        jnp.where(list_positions[None, :] == listed[:, None], values[:, None], 0.0), axis=0
    )
    group_values = lax.psum(spread, "dev")
    slot_energies = jnp.sum(jnp.where(select, group_values[None, :], 0.0), axis=1)
    energy_sum = lax.psum(jnp.sum(group_values), "grp")
    return (slot_energies, energy_sum)


def solution(mesh):
    placed = (
        P(("grp", "dev"), None, None),
        P(("grp", "dev"), None, None),
        P(("grp", "dev"), None, None),
        P("dev", None, None),
        P(("grp", "dev"), None, None),
        P(),
        P(),
        P(),
    )
    return jax.shard_map(
        on_device, mesh=mesh, in_specs=placed, out_specs=(P(("grp", "dev")), P()), check_vma=False
    )
```

profile of v0, /device:TPU:0, one launch (start us, length us, event | category | flops | bytes accessed | tf_op | source)
XLA Modules:
  0.0 507.8 jit_solution(12127098727024818767)
XLA Ops:
  7.2 34.1 %all_gather.9 = bf16[8,200,200]{2,1,0:T(8,128)(2,1)S(1)} all-gather(bf16[1,200,200]{2,1,0:T(8,128)(2,1)} %param.10), channel_id=1, replica_groups=mesh['grp'=4,'dev'=8] {'dev'}, dimensions={0}, use_global_device_ids=true | all-gather | bytes 720000 | tf_op jit(solution)/shard_map/all_gather | solution.py:78
  41.4 5.0 reshape.86
  46.3 6.2 %dot_general.108 = bf16[200,200,24]{1,0,2:T(8,128)(2,1)} reshape(bf16[40000,24]{0,1:T(8,128)(2,1)} %bitcast.141) | data formatting | bytes 3840000 | tf_op jit(solution)/shard_map/dot_general | solution.py:84
  52.5 4.5 fusion.43
  57.1 2.2 copy.39
  59.4 58.9 %reduce-scatter.2.cloned.1.call-done = bf16[1,200,200]{2,1,0:T(8,128)(2,1)} async-done(((bf16[8,200,200]{2,1,0:T(8,128)(2,1)}), bf16[1,200,200]{2,1,0:T(8,128)(2,1)}) %reduce-scatter.2.cloned.1.call-update) | async-done | bytes 80016 | tf_op jit(solution)/shard_map/reduce_scatter | solution.py:83
  120.1 1.3 collective-permute-start
  121.4 2.2 collective-permute-done
  124.4 1.3 copy.42
  126.9 37.5 %all-gather.3.cloned.1.call-done = bf16[8,2,200,200]{3,2,1,0:T(8,128)(2,1)} async-done(((bf16[1,2,200,200]{3,2,1,0:T(8,128)(2,1)}), bf16[8,2,200,200]{3,2,1,0:T(8,128)(2,1)}) %all-gather.3.cloned.1.call-update) | async-done | bytes 1280016 | tf_op jit(solution)/shard_map/all_gather | solution.py:98
  164.4 3.0 copy.40
  167.4 50.4 %all-gather.5.cloned.1.call-done = bf16[8,3,200,200]{3,2,1,0:T(8,128)(2,1)} async-done(((bf16[1,3,200,200]{3,2,1,0:T(8,128)(2,1)}), bf16[8,3,200,200]{3,2,1,0:T(8,128)(2,1)}) %all-gather.5.cloned.1.call-update) | async-done | bytes 1920016 | tf_op jit(solution)/shard_map/all_gather | solution.py:99
  217.7 257.0 %while.12 = (s32[]{:T(128)}, f32[12]{0:T(128)S(1)}, s32[12]{0:T(128)S(1)}, s32[96,2]{0,1:T(2,128)S(1)}, s32[32]{0:T(128)S(1)}, /*index=5*/s32[]{:T(128)}, bf16[8...) while((s32[]{:T(128)}, f32[12]{0:T(128)S(1)}, ...), condition=%wide.region_6.7_spmd, body=%wide.region_2.6_spmd.sunk | while | flops 550840000 | bytes 10257487 | solution.py:132
  227.8 1.7 multiply_reduce_fusion.3
  249.3 1.7 multiply_reduce_fusion.3
  270.7 1.7 multiply_reduce_fusion.3
  273.5 1.1 fusion.135
  292.1 1.7 multiply_reduce_fusion.3
  294.9 1.1 fusion.135
  313.5 1.7 multiply_reduce_fusion.3
  316.3 1.1 fusion.135
  334.9 1.7 multiply_reduce_fusion.3
  356.3 1.7 multiply_reduce_fusion.3
  359.2 1.1 fusion.135
  377.7 1.7 multiply_reduce_fusion.3
  399.1 1.7 multiply_reduce_fusion.3
  420.5 1.7 multiply_reduce_fusion.3
  423.4 1.1 fusion.135
  441.9 1.7 multiply_reduce_fusion.3
  463.4 1.7 multiply_reduce_fusion.3
  474.8 19.0 %psum.14 = f32[96]{0:T(128)S(1)} all-reduce(f32[96]{0:T(128)S(1)} %select_reduce_fusion.1), channel_id=1, replica_groups=mesh['grp'=4,'dev'=8] {'dev'}, use_global_device_ids=true, to_apply=%region_8.9 | all-reduce | flops 96 | bytes 768 | tf_op jit(solution)/shard_map/psum | solution.py:136
  495.0 6.3 %psum.15 = f32[]{:T(128)} all-reduce(f32[]{:T(128)} %reduce_sum.65), channel_id=1, replica_groups=mesh['grp'=4,'dev'=8] {'grp'}, use_global_device_ids=true, to_apply=%region_11.12 | all-reduce | flops 1 | bytes 8 | tf_op jit(solution)/shard_map/psum | solution.py:138
  (319 shorter events, 129.3 us)
Async XLA Ops:
  7.2 119.6 %copy-start = (s32[384,2]{0,1:T(2,128)S(1)}, s32[384,2]{0,1:T(2,128)}, u32[]{:S(2)}) copy-start(s32[384,2]{0,1:T(2,128)} %param.15) | copy-start | bytes 9220
  7.2 111.1 %reduce-scatter.2.cloned.1.call-start = ((), (), s32[]{:S(2)}) async-start(), calls=%async_computation.1 | async-start | bytes 921600 | tf_op jit(solution)/shard_map/reduce_scatter | solution.py:83
  46.3 6.2 %copy-start.1 = (bf16[24,200,200]{2,1,0:T(8,128)(2,1)S(1)}, bf16[24,200,200]{2,1,0:T(8,128)(2,1)}, u32[]{:S(2)}) copy-start(bf16[24,200,200]{2,1,0:T(8,128)(2,1)} %param.13) | copy-start | bytes 5760004
  57.1 61.2 %copy-start.5 = (bf16[1,200,200]{2,1,0:T(8,128)(2,1)S(1)}, bf16[1,200,200]{2,1,0:T(8,128)(2,1)}, u32[]{:S(2)}) copy-start(bf16[1,200,200]{2,1,0:T(8,128)(2,1)} %param.12) | copy-start | bytes 240004
  57.1 61.2 %copy-start.6 = (bf16[1,200,200]{2,1,0:T(8,128)(2,1)S(1)}, bf16[1,200,200]{2,1,0:T(8,128)(2,1)}, u32[]{:S(2)}) copy-start(bf16[1,200,200]{2,1,0:T(8,128)(2,1)} %param.11) | copy-start | bytes 240004
  57.1 62.2 %copy-start.3 = (bf16[1,200,200]{2,1,0:T(8,128)(2,1)S(1)}, bf16[1,200,200]{2,1,0:T(8,128)(2,1)}, u32[]{:S(2)}) copy-start(bf16[1,200,200]{2,1,0:T(8,128)(2,1)} %param.14) | copy-start | bytes 240004
  57.1 63.0 %copy-start.2 = (bf16[1,200,200]{2,1,0:T(8,128)(2,1)S(1)}, bf16[1,200,200]{2,1,0:T(8,128)(2,1)}, u32[]{:S(2)}) copy-start(bf16[1,200,200]{2,1,0:T(8,128)(2,1)} %param.10) | copy-start | bytes 240004
  59.3 105.0 %all-gather.3.cloned.1.call-start = ((), (), s32[]{:S(2)}) async-start(), calls=%async_computation.2 | async-start | bytes 1843200 | tf_op jit(solution)/shard_map/all_gather | solution.py:98
  120.0 97.7 %all-gather.5.cloned.1.call-start = ((), (), s32[]{:S(2)}) async-start(), calls=%async_computation.3 | async-start | bytes 2764800 | tf_op jit(solution)/shard_map/all_gather | solution.py:99
  120.1 3.5 collective-permute-start
  123.6 0.7 copy-start.4
  126.9 90.9 %copy-start.7 = (s32[32]{0:T(128)S(1)}, s32[32]{0:T(128)}, u32[]{:S(2)}) copy-start(s32[32]{0:T(128)} %param.17) | copy-start | bytes 388
Sparse Core Ops, SparseCore 0:
  59.5 58.7 reduce-scatter.1
  120.5 43.8 all-gather.2
  166.5 51.1 all-gather.4
where the time goes:
time: 511 us; the launch traced here: 508 us
  waiting for transfers between devices  149 us (29%)
  loops' own time  107 us (21%)
  matrix products  81.2 us (16%)
  local copies, waits for them, and re-layouts  60.5 us (12%)
  blocking collectives  59.4 us (12%)
  other arithmetic  35.9 us (7%)
  between operations  13.8 us (3%)
    another operation x1, loops' own time, on_device(): values = lax.map(energy_of, listed)  107 us
    dot_general x144, matrix products, product(): return jnp.dot(left, right, preferred_element_type=jnp.float32)  76.7 us
    reduce_scatter x1, waiting for transfers between devices, on_device(): lax.psum_scatter(jnp.dot(coeffs, flat_fit, preferred_element_type=jnp.flo...  58.9 us
    all_gather x1, waiting for transfers between devices, on_device(): lax.all_gather(following, 'dev', axis=0, tiled=True)  50.4 us
    all_gather x1, waiting for transfers between devices, on_device(): lax.all_gather(local_pair, 'dev', axis=0, tiled=True)  37.5 us
    all_gather x1, blocking collectives, on_device(): gathered = lax.all_gather(densities, 'dev', axis=0, tiled=True)  34.1 us
    reduce_sum x12, other arithmetic, dimer_energy(): monomer_j = jnp.sum(dens_j.astype(jnp.float32) * fock_j.astype(jnp.float32))  20.7 us
    psum x1, blocking collectives, on_device(): group_values = lax.psum(spread, 'dev')  19 us
  transfers between devices with their start and end apart: 4, of which 4 were waited for; matrix products, arithmetic and copies ran while one was open for 1% of the time, Pallas kernels for 0%

commit v1 on v0

v1 whole, which is shorter than its diff:
```python
import jax
import jax.numpy as jnp
from jax import lax
from jax.sharding import PartitionSpec as P

SLOTS = 24
F32 = jnp.float32
BF = jnp.bfloat16


def dot(left, right, dims=((1,), (0,))):
    return lax.dot_general(left, right, (dims, ((), ())), preferred_element_type=F32)


def lookup(table, mono, pairs, assignment, owner_map, group, member, members, groups):
    count = pairs.shape[0]
    per_group = count // groups
    rows = members * groups
    frag_ids = jnp.arange(rows, dtype=jnp.int32)
    row_of = lambda frag: jnp.sum(
        jnp.where(frag[:, None] == frag_ids[None, :], owner_map[None, :], 0), axis=1
    )
    first, second = row_of(pairs[:, 0]), row_of(pairs[:, 1])
    column = second - (jnp.arange(count, dtype=jnp.int32) // per_group) * members
    table_rows = jnp.sum(
        jnp.where((first[:, None] == frag_ids[None, :])[:, :, None], table[None, :, :], 0.0), axis=1
    )
    columns = jnp.arange(2 * members, dtype=jnp.int32)
    energies = jnp.sum(jnp.where(column[:, None] == columns[None, :], table_rows, 0.0), axis=1)
    energies = energies + jnp.sum(
        jnp.where(second[:, None] == frag_ids[None, :], mono[None, :], 0.0), axis=1
    )
    start = group * per_group
    mine = lax.dynamic_slice_in_dim(assignment, start, per_group, 0) == member
    mine_count = mine.astype(jnp.int32)
    before = jnp.cumsum(mine_count) - mine_count
    select = mine[None, :] & (before[None, :] == jnp.arange(SLOTS, dtype=jnp.int32)[:, None])
    own = lax.dynamic_slice_in_dim(energies, start, per_group, 0)
    return jnp.sum(jnp.where(select, own[None, :], 0.0), axis=1), jnp.sum(energies)


def on_device(dens, core, embed, fit, ortho, pairs, assignment, owner_map):
    members, groups = lax.axis_size("dev"), lax.axis_size("grp")
    group, member = lax.axis_index("grp"), lax.axis_index("dev")
    basis = dens.shape[1]
    aux = fit.shape[0]
    flat_fit = fit.reshape(aux, basis * basis)
    gathered = lax.all_gather(dens, "dev", axis=0, tiled=True)
    coeffs = dot(gathered.reshape(members, basis * basis), flat_fit, ((1,), (1,))).astype(BF)
    coulomb = lax.psum_scatter(
        dot(coeffs, flat_fit).reshape(members, basis, basis).astype(BF),
        "dev",
        scatter_dimension=0,
        tiled=True,
    ).astype(F32)
    fock = (core.astype(F32) + embed.astype(F32) + coulomb).astype(BF)[0]
    d, x = dens[0], ortho[0]
    v = dot(fock, x).astype(BF)
    u = dot(d, x).astype(BF)
    xf = dot(x, fock, ((0,), (0,))).astype(BF)
    xd = dot(x, d, ((0,), (0,))).astype(BF)
    a = dot(x, v, ((0,), (0,)))
    a_sym = (0.5 * (a + a.T)).astype(BF)
    ab = a.astype(BF)
    mono = (
        0.5 * jnp.trace(a)
        - 0.1875 * jnp.sum(a * a)
        + jnp.sum(dot(ab, ab) * dot(ab, ab, ((1,), (1,)))) / 256.0
        - jnp.sum(d.astype(F32) * fock.astype(F32))
    )
    block = jnp.stack([u, v, a_sym])[None]
    own_pool = lax.all_gather(block, "dev", axis=0, tiled=True)
    route = [(g, (g - 1) % groups) for g in range(groups)]
    next_pool = lax.ppermute(own_pool, "grp", route)
    pool = jnp.concatenate([own_pool, next_pool], axis=0)

    def pair_term(entry):
        u_j, v_j, c_sym = entry[0], entry[1], entry[2]
        b = 0.5 * (dot(xf, u_j) + dot(xd, v_j))
        bb = b.astype(BF)
        left, right, gram = dot(a_sym, bb), dot(bb, c_sym), dot(bb, bb, ((1,), (1,)))
        both = left + right
        quartic = left * left + right * right + both * both + gram * gram
        return jnp.sum(quartic / 128.0 - 0.375 * (b * b))

    terms = lax.map(pair_term, pool)
    line = jnp.concatenate([terms + mono, mono[None]])
    table = lax.all_gather(line[None], ("grp", "dev"), axis=0, tiled=True)
    return lookup(
        table[:, :-1], table[:, -1], pairs, assignment, owner_map, group, member, members, groups
    )


def solution(mesh):
    rows = P(("grp", "dev"), None, None)
    placed = (rows, rows, rows, P("dev", None, None), rows, P(), P(), P())
    return jax.shard_map(
        on_device, mesh=mesh, in_specs=placed, out_specs=(P(("grp", "dev")), P()), check_vma=False
    )
```

time: 511 us -> 340 us (0.67)
  loops' own time: 107 us -> 0.4 us
  local copies, waits for them, and re-layouts: 60.5 us -> 25 us
  other arithmetic: 35.9 us -> 10.5 us
  blocking collectives: 59.4 us -> 75.5 us
  waiting for transfers between devices: 149 us -> 133 us
    another operation x1, loops' own time: 107 us -> 0.4 us  [on_device(): terms = lax.map(pair_term, pool)]
    unnamed x0 -> x1, blocking collectives: none -> 39.4 us
    all_gather x2 -> x1, waiting for transfers between devices: 87.8 us -> 52 us  [on_device(): own_pool = lax.all_gather(block, 'dev', axis=0, tiled=True)]
    reduce_sum x27 -> x8, other arithmetic: 32.9 us -> 3.88 us  [the longest x1 1.56 us: on_device(): jnp.sum(d.astype(F32) * fock.astype(F32))]
    psum x2 -> x0, blocking collectives: 25.2 us -> none  [the longest x1 19 us: on_device(): group_values = lax.psum(spread, 'dev')]
    ppermute x1, waiting for transfers between devices: 2.19 us -> 22.2 us  [on_device(): next_pool = lax.ppermute(own_pool, 'grp', route)]
    slice x24 -> x2, local copies, waits for them, and re-layouts: 19.3 us -> 0.2 us  [the longest x1 0.18 us: on_device(): table[:, -1]]
    dynamic_slice x37 -> x1, local copies, waits for them, and re-layouts: 16.6 us -> 0.07 us  [lookup(): own = lax.dynamic_slice_in_dim(energies, start, per_group, 0)]
  transfers between devices with their start and end apart: 4 -> 3, of which waited for: 4 -> 3; matrix products, arithmetic and copies ran while one was open for 1% -> 1% of each run, Pallas kernels for 0% -> 0%
where the time goes in v1:
time: 340 us; the launch traced here: 338 us
  waiting for transfers between devices  133 us (39%)
  matrix products  76.3 us (22%)
  blocking collectives  75.5 us (22%)
  local copies, waits for them, and re-layouts  25 us (7%)
  between operations  16.9 us (5%)
  other arithmetic  10.5 us (3%)
    dot_general x88, matrix products, dot(): lax.dot_general(left, right, (dims, ((), ())), preferred_element_type=F32)  76.3 us
    reduce_scatter x1, waiting for transfers between devices, on_device(): lax.psum_scatter(dot(coeffs, flat_fit).reshape(members, basis, basis).ast...  58.7 us
    all_gather x1, waiting for transfers between devices, on_device(): own_pool = lax.all_gather(block, 'dev', axis=0, tiled=True)  52 us
    unnamed x1, blocking collectives  39.4 us
    all_gather x1, blocking collectives, on_device(): gathered = lax.all_gather(dens, 'dev', axis=0, tiled=True)  36.1 us
    ppermute x1, waiting for transfers between devices, on_device(): next_pool = lax.ppermute(own_pool, 'grp', route)  22.2 us
    dynamic_update_slice x16, local copies, waits for them, and re-layouts, on_device(): terms = lax.map(pair_term, pool)  12.1 us
  transfers between devices with their start and end apart: 3, of which 3 were waited for; matrix products, arithmetic and copies ran while one was open for 1% of the time, Pallas kernels for 0%

profile of v1, /device:TPU:0, one launch (start us, length us, event | category | flops | bytes accessed | tf_op | source)
XLA Modules:
  0.0 337.6 jit_solution(6582617387170707575)
XLA Ops:
  7.2 5.0 %reshape.89 = bf16[24,40000]{1,0:T(8,128)(2,1)} reshape(bf16[24,200,200]{2,1,0:T(8,128)(2,1)} %param.13) | data formatting | bytes 3840000 | tf_op jit(solution)/shard_map/reshape | solution.py:47
  12.2 6.2 %dot_general.53 = bf16[200,200,24]{1,0,2:T(8,128)(2,1)} reshape(bf16[40000,24]{0,1:T(8,128)(2,1)} %bitcast.123) | data formatting | bytes 3840000 | tf_op jit(solution)/shard_map/dot_general | solution.py:12
  18.4 36.1 %all_gather.9 = bf16[8,200,200]{2,1,0:T(8,128)(2,1)} all-gather(bf16[1,200,200]{2,1,0:T(8,128)(2,1)S(1)} %copy-done.2), channel_id=1, replica_groups=mesh['grp'=4,'dev'=8] {'dev'}, dimensions={0}, use_global_device_ids=true | all-gather | bytes 720000 | tf_op jit(solution)/shard_map/all_gather | solution.py:48
  54.5 3.9 %fusion.17 = bf16[8,200,200]{2,0,1:T(8,128)(2,1)S(1)} fusion(bf16[200,200,24]{1,0,2:T(8,128)(2,1)} %dot_general.53, bf16[24,200,200]{2,1,0:T(8,128)(2,1)S(1)} %copy-done.1, bf16[8,200,200]{2,1,0:T(8,128)(2,1)} %all_gather.9), kind=kOutput, calls=%fused_computation.24 | convolution fusion | flops 31040192 | bytes 5120000 | tf_op jit(solution)/shard_map/dot_general | solution.py:12
  59.7 58.7 %reduce-scatter.2.cloned.1.call-done = bf16[1,200,200]{2,1,0:T(8,128)(2,1)} async-done(((bf16[8,200,200]{2,1,0:T(8,128)(2,1)}), bf16[1,200,200]{2,1,0:T(8,128)(2,1)}) %reduce-scatter.2.cloned.1.call-update) | async-done | bytes 80016 | tf_op jit(solution)/shard_map/reduce_scatter | solution.py:50
  118.4 1.6 multiply_reduce_fusion
  122.0 52.0 %all-gather.4.cloned.1.call-done = bf16[24,200,200]{2,1,0:T(8,128)(2,1)} async-done(((bf16[3,200,200]{2,1,0:T(8,128)(2,1)}), bf16[24,200,200]{2,1,0:T(8,128)(2,1)}) %all-gather.4.cloned.1.call-update) | async-done | bytes 1920016 | tf_op jit(solution)/shard_map/all_gather | solution.py:72
  179.5 22.2 %collective-permute-done = bf16[8,3,200,200]{3,2,1,0:T(8,128)(2,1)S(1)} collective-permute-done((bf16[8,3,200,200]{3,2,1,0:T(8,128)(2,1)}, bf16[8,3,200,200]{3,2,1,0:T(8,128)(2,1)S(1)}, u32[]{:S(2)}, u32[]{:S(2)}) %collective-permute-start) | collective-permute-done | bytes 1920032 | tf_op jit(solution)/shard_map/ppermute | solution.py:74
  201.7 4.7 %pad_maximum_fusion = bf16[16,3,200,200]{3,2,1,0:T(8,128)(2,1)} fusion(bf16[8,3,200,200]{3,2,1,0:T(8,128)(2,1)S(1)} %collective-permute-done, bf16[8,3,200,200]{3,2,1,0:T(8,128)(2,1)} %bitcast.126), kind=kLoop, calls=%fused_computation.19 | loop fusion | flops 1920000 | bytes 7680000 | tf_op jit(solution)/shard_map/concatenate | solution.py:75
  206.4 82.9 %while.10 = (s32[]{:T(128)}, f32[16]{0:T(128)S(1)}, bf16[16,3,200,200]{3,2,1,0:T(8,128)(2,1)}, bf16[200,200]{1,0:T(8,128)(2,1)S(1)}, bf16[200,200]{1,0:T(8,128)(...) while((s32[]{:T(128)}, f32[16]{0:T(128)S(1)}, ...), condition=%wide.region_6.7_spmd, body=%wide.region_4.6_spmd.sunk | while | flops 80720000 | bytes 2147369 | solution.py:86
  208.9 1.1 fusion.95
  214.0 1.1 fusion.95
  219.2 1.1 fusion.95
  224.4 1.1 fusion.95
  228.3 1.1 fusion.94
  229.6 1.1 fusion.95
  233.5 1.1 fusion.94
  234.8 1.1 fusion.95
  238.6 1.1 fusion.94
  240.0 1.1 fusion.95
  243.8 1.1 fusion.94
  245.2 1.1 fusion.95
  250.3 1.1 fusion.95
  255.5 1.1 fusion.95
  260.7 1.1 fusion.95
  265.9 1.1 fusion.95
  271.1 1.1 fusion.95
  276.2 1.1 fusion.95
  280.1 1.1 fusion.94
  281.4 1.1 fusion.95
  286.6 1.1 fusion.95
  289.5 39.4 %all-reduce = f32[544]{0:T(1024)S(1)} all-reduce(f32[544]{0:T(1024)S(1)} %maximum_dynamic-update-slice_fusion), channel_id=3, replica_groups=mesh['grp'=4,'dev'=8] {'grp','dev'}, use_global_device_ids=true, to_apply=%add | all-reduce | flops 544 | bytes 4352
  (129 shorter events, 67.0 us)
Async XLA Ops:
  7.2 52.4 %copy-start = (bf16[1,200,200]{2,1,0:T(8,128)(2,1)S(1)}, bf16[1,200,200]{2,1,0:T(8,128)(2,1)}, u32[]{:S(2)}) copy-start(bf16[1,200,200]{2,1,0:T(8,128)(2,1)} %param.14) | copy-start | bytes 240004
  7.2 111.2 %reduce-scatter.2.cloned.1.call-start = ((), (), s32[]{:S(2)}) async-start(), calls=%async_computation.1 | async-start | bytes 921600 | tf_op jit(solution)/shard_map/reduce_scatter | solution.py:50
  12.2 6.2 %copy-start.2 = (bf16[1,200,200]{2,1,0:T(8,128)(2,1)S(1)}, bf16[1,200,200]{2,1,0:T(8,128)(2,1)}, u32[]{:S(2)}) copy-start(bf16[1,200,200]{2,1,0:T(8,128)(2,1)} %param.10) | copy-start | bytes 240004
  12.2 42.3 %copy-start.1 = (bf16[24,200,200]{2,1,0:T(8,128)(2,1)S(1)}, bf16[24,200,200]{2,1,0:T(8,128)(2,1)}, u32[]{:S(2)}) copy-start(bf16[24,200,200]{2,1,0:T(8,128)(2,1)} %param.13) | copy-start | bytes 5760004
  58.4 60.1 %copy-start.4 = (bf16[1,200,200]{2,1,0:T(8,128)(2,1)S(1)}, bf16[1,200,200]{2,1,0:T(8,128)(2,1)}, u32[]{:S(2)}) copy-start(bf16[1,200,200]{2,1,0:T(8,128)(2,1)} %param.12) | copy-start | bytes 240004
  58.4 60.0 %copy-start.5 = (bf16[1,200,200]{2,1,0:T(8,128)(2,1)S(1)}, bf16[1,200,200]{2,1,0:T(8,128)(2,1)}, u32[]{:S(2)}) copy-start(bf16[1,200,200]{2,1,0:T(8,128)(2,1)} %param.11) | copy-start | bytes 240004
  59.4 115.7 %copy-start.6 = (s32[384,2]{0,1:T(2,128)S(1)}, s32[384,2]{0,1:T(2,128)}, u32[]{:S(2)}) copy-start(s32[384,2]{0,1:T(2,128)} %param.15) | copy-start | bytes 9220
  59.4 115.7 %copy-start.7 = (s32[32]{0:T(128)S(1)}, s32[32]{0:T(128)}, u32[]{:S(2)}) copy-start(s32[32]{0:T(128)} %param.17) | copy-start | bytes 388
  59.5 115.9 %copy-start.3 = (bf16[1,200,200]{2,1,0:T(8,128)(2,1)S(1)}, bf16[1,200,200]{2,1,0:T(8,128)(2,1)}, u32[]{:S(2)}) copy-start(bf16[1,200,200]{2,1,0:T(8,128)(2,1)} %param.10) | copy-start | bytes 240004
  59.5 114.5 %all-gather.4.cloned.1.call-start = ((), (), s32[]{:S(2)}) async-start(), calls=%async_computation.2 | async-start | bytes 2764800 | tf_op jit(solution)/shard_map/all_gather | solution.py:72
  174.0 27.7 %collective-permute-start = (bf16[8,3,200,200]{3,2,1,0:T(8,128)(2,1)}, bf16[8,3,200,200]{3,2,1,0:T(8,128)(2,1)S(1)}, u32[]{:S(2)}, u32[]{:S(2)}) collective-permute-start(bf16[8,3,200,200]{3,2,1,0:T(8,128)(2,1)} %bitcast.125), channel_id=1, source_target_pairs={{0,24},{8,0},{16,8},{24,16},{1,25},{9,1},{17,9},{25,17},{2,26},{10... | collective-permute-start | bytes 5760008 | tf_op jit(solution)/shard_map/ppermute | solution.py:74
Sparse Core Ops, SparseCore 0:
  59.6 58.7 reduce-scatter.1
  122.2 51.7 all-gather.3

commit v2 on v1

v2 whole, which is shorter than its diff:
```python
import functools

import jax
import jax.numpy as jnp
from jax import lax
from jax.experimental import pallas as pl
from jax.experimental.pallas import tpu as pltpu
from jax.sharding import PartitionSpec as P

SLOTS = 24
F32 = jnp.float32
BF = jnp.bfloat16
MESH = pl.DeviceIdType.MESH
MONO_LANE = 127


def dot(left, right, dims=((1,), (0,))):
    return lax.dot_general(left, right, (dims, ((), ())), preferred_element_type=F32)


def lookup(table, mono, pairs, assignment, owner_map, group, member, members, groups):
    count = pairs.shape[0]
    per_group = count // groups
    rows = members * groups
    frag_ids = jnp.arange(rows, dtype=jnp.int32)
    row_of = lambda frag: jnp.sum(
        jnp.where(frag[:, None] == frag_ids[None, :], owner_map[None, :], 0), axis=1
    )
    first, second = row_of(pairs[:, 0]), row_of(pairs[:, 1])
    column = second - (jnp.arange(count, dtype=jnp.int32) // per_group) * members
    table_rows = jnp.sum(
        jnp.where((first[:, None] == frag_ids[None, :])[:, :, None], table[None, :, :], 0.0), axis=1
    )
    columns = jnp.arange(2 * members, dtype=jnp.int32)
    energies = jnp.sum(jnp.where(column[:, None] == columns[None, :], table_rows, 0.0), axis=1)
    energies = energies + jnp.sum(
        jnp.where(second[:, None] == frag_ids[None, :], mono[None, :], 0.0), axis=1
    )
    start = group * per_group
    mine = lax.dynamic_slice_in_dim(assignment, start, per_group, 0) == member
    mine_count = mine.astype(jnp.int32)
    before = jnp.cumsum(mine_count) - mine_count
    select = mine[None, :] & (before[None, :] == jnp.arange(SLOTS, dtype=jnp.int32)[:, None])
    own = lax.dynamic_slice_in_dim(energies, start, per_group, 0)
    return jnp.sum(jnp.where(select, own[None, :], 0.0), axis=1), jnp.sum(energies)


def row_chunks(rows, size=32):
    return [(at, min(size, rows - at)) for at in range(0, rows, size)]


def kernel(
    members, groups, dens, core, embed, fit, ortho, table_out,
    dens_pool, ortho_pool, fock_pool, coef, part, inbox, own, sums, table,
    send, recv, part_send, part_recv, row_send, row_recv,
):
    n, half = members, members // 2
    total = members * groups
    basis, aux = fit.shape[1], fit.shape[0]
    group, member = lax.axis_index("grp"), lax.axis_index("dev")
    me = group * n + member
    partner = member + 1 - 2 * lax.rem(member, 2)
    before = lax.rem(group + groups - 1, groups)
    pools = (dens_pool, ortho_pool, fock_pool)

    def other(k):
        flat = lax.rem(me + k, total)
        return (lax.div(flat, n), lax.rem(flat, n))

    def loop(low, high, step):
        def run(k, carry):
            step(k)
            return carry

        lax.fori_loop(low, high, run, 0)

    barrier = pltpu.get_barrier_semaphore()
    loop(
        1,
        total,
        lambda k: pl.semaphore_signal(barrier, inc=1, device_id=other(k), device_id_type=MESH),
    )
    pl.semaphore_wait(barrier, total - 1)

    def remote(src, dst, send_sem, recv_sem, device):
        return pltpu.make_async_remote_copy(
            src_ref=src,
            dst_ref=dst,
            send_sem=send_sem,
            recv_sem=recv_sem,
            device_id=device,
            device_id_type=MESH,
        )

    def ship(m, src, slot, send_slot, device):
        remote(src, pools[m].at[slot], send.at[m, send_slot], recv.at[m, slot], device).start()

    def arrived(m, slot):
        pool = pools[m]
        remote(
            pool.at[slot], pool.at[slot], send.at[m, 0], recv.at[m, slot], (group, partner)
        ).wait_recv()

    def start_own(m, src):
        for k in range(1, half):
            ship(m, src, member, k - 1, (group, lax.rem(member + 2 * k, n)))
        ship(m, src, member, half - 1, (group, partner))
        ship(m, src, n + member, n - 1, (before, member))

    def take_line(m, k):
        slot = lax.rem(member + 2 * k, n)
        arrived(m, slot)
        ship(m, pools[m].at[slot], slot, half - 1 + k, (group, partner))
        ship(m, pools[m].at[slot], n + slot, n - 1 + k, (before, member))
        return slot

    def take_partner(m, k):
        slot = lax.rem(partner + 2 * k, n)
        arrived(m, slot)
        ship(m, pools[m].at[slot], n + slot, n - 1 + half + k, (before, member))
        return slot

    dens_pool[member] = dens[0]
    ortho_pool[member] = ortho[0]
    start_own(0, dens.at[0])
    loop(1, half, lambda k: take_line(0, k))
    start_own(1, ortho.at[0])
    loop(0, half, lambda k: take_partner(0, k))

    def coefficients(p):
        totals = [jnp.zeros((8, basis), F32) for _ in range(n)]
        for at, size in row_chunks(basis):
            factor = fit[p, at : at + size, :].astype(F32)
            for f in range(n):
                prod = dens_pool[f, at : at + size, :].astype(F32) * factor
                totals[f] = totals[f] + jnp.sum(prod.reshape(size // 8, 8, basis), axis=0)
        stacked = jnp.concatenate([jnp.sum(t, axis=0, keepdims=True) for t in totals], axis=0)
        value = jnp.sum(stacked, axis=1, keepdims=True).astype(BF).astype(F32)
        coef[p] = jnp.broadcast_to(value, (n, basis))

    loop(0, aux, coefficients)
    loop(1, half, lambda k: take_line(1, k))

    def partial(slot, at, size):
        value = jnp.zeros((size, basis), F32)
        for p in range(aux):
            value = value + coef[p, pl.ds(slot, 1), :] * fit[p, at : at + size, :].astype(F32)
        return value

    def send_part(k):
        slot = lax.rem(member + k, n)
        for at, size in row_chunks(basis):
            part[k, at : at + size, :] = partial(slot, at, size).astype(BF)
        remote(
            part.at[k], inbox.at[k], part_send.at[k], part_recv.at[k], (group, slot)
        ).start()

    loop(1, n, send_part)
    for at, size in row_chunks(basis):
        sums[at : at + size, :] = (
            partial(member, at, size)
            + core[0, at : at + size, :].astype(F32)
            + embed[0, at : at + size, :].astype(F32)
        )
    loop(0, half, lambda k: take_partner(1, k))

    def add_part(k):
        remote(
            part.at[k], inbox.at[k], part_send.at[k], part_recv.at[k], (group, partner)
        ).wait()
        sums[...] += inbox[k].astype(F32)

    loop(1, n, add_part)
    fock_pool[member] = sums[...].astype(BF)
    start_own(2, fock_pool.at[member])

    fock, d, x = fock_pool[member], dens[0], ortho[0]
    v = dot(fock, x).astype(BF)
    own[0] = (0.5 * dot(x, fock, ((0,), (0,)))).astype(BF)
    own[1] = (0.5 * dot(x, d, ((0,), (0,)))).astype(BF)
    a = dot(x, v, ((0,), (0,)))
    own[2] = (0.5 * (a + a.T)).astype(BF)
    ab = a.astype(BF)
    on_diagonal = lax.broadcasted_iota(jnp.int32, a.shape, 0) == lax.broadcasted_iota(
        jnp.int32, a.shape, 1
    )
    terms = (
        jnp.where(on_diagonal, 0.5 * a, 0.0)
        - 0.1875 * (a * a)
        + dot(ab, ab) * dot(ab, ab, ((1,), (1,))) * (1.0 / 256.0)
        - d.astype(F32) * fock.astype(F32)
    )
    mono = jnp.sum(jnp.sum(terms, axis=0, keepdims=True), axis=1, keepdims=True)

    lanes = lax.broadcasted_iota(jnp.int32, (1, 128), 1)
    table[me] = jnp.where(lanes == MONO_LANE, mono, 0.0)

    def pair(slot):
        x_j = ortho_pool[slot]
        u_j = dot(dens_pool[slot], x_j).astype(BF)
        v_j = dot(fock_pool[slot], x_j).astype(BF)
        c = dot(x_j, v_j, ((0,), (0,)))
        c_sym = (0.5 * (c + c.T)).astype(BF)
        b = dot(own[0], u_j) + dot(own[1], v_j)
        bb = b.astype(BF)
        left, right, gram = dot(own[2], bb), dot(bb, c_sym), dot(bb, bb, ((1,), (1,)))
        both = left + right
        quartic = left * left + right * right + both * both + gram * gram
        terms = quartic * (1.0 / 128.0) - 0.375 * (b * b)
        value = jnp.sum(jnp.sum(terms, axis=0, keepdims=True), axis=1, keepdims=True)
        table[me] = table[me] + jnp.where(lanes == slot, value + mono, 0.0)

    loop(1, half, lambda k: pair(take_line(2, k)))
    loop(0, half, lambda k: pair(take_partner(2, k)))

    def next_pair(k):
        slot = n + lax.rem(member + k, n)
        for m in range(3):
            arrived(m, slot)
        pair(slot)

    loop(0, n, next_pair)

    def send_row(k):
        remote(table.at[me], table.at[me], row_send.at[k], row_recv.at[k], other(k)).start()

    def take_row(k):
        source = lax.rem(me + total - k, total)
        remote(
            table.at[me], table.at[source], row_send.at[k], row_recv.at[k], other(k)
        ).wait()

    loop(1, total, send_row)
    loop(1, total, take_row)
    table_out[...] = table[...]

    def sent(k):
        for m in range(3):
            pool = pools[m]
            remote(
                pool.at[0], pool.at[0], send.at[m, k], recv.at[m, 0], (group, partner)
            ).wait_send()

    loop(0, 2 * n - 1, sent)


def on_device(dens, core, embed, fit, ortho, pairs, assignment, owner_map):
    members, groups = lax.axis_size("dev"), lax.axis_size("grp")
    group, member = lax.axis_index("grp"), lax.axis_index("dev")
    basis, aux = dens.shape[1], fit.shape[0]
    total = members * groups
    square = (basis, basis)
    dma = pltpu.SemaphoreType.DMA
    vmem = pl.BlockSpec(memory_space=pltpu.VMEM)
    table = pl.pallas_call(
        functools.partial(kernel, members, groups),
        out_shape=jax.ShapeDtypeStruct((total, 1, 128), F32),
        in_specs=[vmem] * 5,
        out_specs=vmem,
        scratch_shapes=[
            pltpu.VMEM((2 * members,) + square, BF),
            pltpu.VMEM((2 * members,) + square, BF),
            pltpu.VMEM((2 * members,) + square, BF),
            pltpu.VMEM((aux, members, basis), F32),
            pltpu.VMEM((members,) + square, BF),
            pltpu.VMEM((members,) + square, BF),
            pltpu.VMEM((3,) + square, BF),
            pltpu.VMEM(square, F32),
            pltpu.VMEM((total, 1, 128), F32),
            dma((3, 2 * members - 1)),
            dma((3, 2 * members)),
            dma((members,)),
            dma((members,)),
            dma((total,)),
            dma((total,)),
        ],
        compiler_params=pltpu.CompilerParams(
            collective_id=0, has_side_effects=True, vmem_limit_bytes=60 * 1024 * 1024
        ),
    )(dens, core, embed, fit, ortho)[:, 0]
    return lookup(
        table[:, : 2 * members],
        table[:, MONO_LANE],
        pairs, assignment, owner_map, group, member, members, groups,
    )


def solution(mesh):
    rows = P(("grp", "dev"), None, None)
    placed = (rows, rows, rows, P("dev", None, None), rows, P(), P(), P())
    return jax.shard_map(
        on_device, mesh=mesh, in_specs=placed, out_specs=(P(("grp", "dev")), P()), check_vma=False
    )
```

time: 340 us -> 92 us (0.27)
  waiting for transfers between devices: 133 us -> 0 us
  Pallas kernels: 0 us -> 85.1 us
  matrix products: 76.3 us -> 0 us
  blocking collectives: 75.5 us -> 0 us
  local copies, waits for them, and re-layouts: 25 us -> 1.86 us
  between operations: 16.9 us -> 0.68 us
  other arithmetic: 10.5 us -> 4 us
    pallas_call x0 -> x1, Pallas kernels: none -> 85.1 us  [on_device(): pl.pallas_call(functools.partial(kernel, members, groups), out_shape=jax....]
    dot_general x88 -> x0, matrix products: 76.3 us -> none  [dot(): lax.dot_general(left, right, (dims, ((), ())), preferred_element_type=F32)]
    reduce_scatter x1 -> x0, waiting for transfers between devices: 58.7 us -> none  [on_device(): lax.psum_scatter(dot(coeffs, flat_fit).reshape(members, basis, basis).ast...]
    all_gather x1 -> x0, waiting for transfers between devices: 52 us -> none  [on_device(): own_pool = lax.all_gather(block, 'dev', axis=0, tiled=True)]
    unnamed x1 -> x0, blocking collectives: 39.4 us -> none
    all_gather x1 -> x0, blocking collectives: 36.1 us -> none  [on_device(): gathered = lax.all_gather(dens, 'dev', axis=0, tiled=True)]
    ppermute x1 -> x0, waiting for transfers between devices: 22.2 us -> none  [on_device(): next_pool = lax.ppermute(own_pool, 'grp', route)]
    dynamic_update_slice x16 -> x0, local copies, waits for them, and re-layouts: 12.1 us -> none  [on_device(): terms = lax.map(pair_term, pool)]
  transfers between devices with their start and end apart: 3 -> 0, of which waited for: 3 -> 0; matrix products, arithmetic and copies ran while one was open for 1% -> 0% of each run, Pallas kernels for 0% -> 0%
where the time goes in v2:
time: 92 us; the launch traced here: 91.6 us
  Pallas kernels  85.1 us (92%)
  other arithmetic  4 us (4%)
  local copies, waits for them, and re-layouts  1.86 us (2%)
    pallas_call x1, Pallas kernels, on_device(): pl.pallas_call(functools.partial(kernel, members, groups), out_shape=jax....  85.1 us

profile of v2, /device:TPU:0, one launch (start us, length us, event | category | flops | bytes accessed | tf_op | source)
XLA Modules:
  0.0 91.6 jit_solution(11162938476909361730)
XLA Ops:
  0.6 0.8 convert_bitcast_fusion
  1.4 0.1 copy.12
  1.5 0.1 reduce-window.9
  1.6 0.1 reduce
  1.8 0.8 slice_reduce_fusion.2
  2.5 0.7 select_reduce_fusion.3
  3.3 85.1 %shard_map.95 = f32[32,1,128]{2,1,0:T(1,128)} custom-call(bf16[1,200,200]{2,1,0:T(8,128)(2,1)} %dens.1, bf16[1,200,200]{2,1,0:T(8,128)(2,1)} %core.1, bf16[1,200,200]{2,1,0:T(8,128)(2,1)} %embed.1, bf16[24,200,200]{2,1,0:T(8,128)(2,1)} %fit.1, bf16[1,200,200]{2,1,0:T(8,128)(2,1)} %ortho.1), custom_call_target="tpu_custom_call" | custom-call | tf_op jit(solution)/shard_map/pallas_call | solution.py:255
  88.4 0.9 select_reduce_fusion
  89.3 0.9 slice_reduce_fusion
  90.2 0.1 select_reduce_fusion.1
  90.3 0.6 fusion.6
  90.9 0.1 dynamic_slice.7
  91.0 0.6 select_reduce_fusion.5
  (4 shorter events, 0.1 us)

commit v3 on v2

--- a/solution.py
+++ b/solution.py
@@ -59,7 +59,8 @@
     basis, aux = fit.shape[1], fit.shape[0]
     group, member = lax.axis_index("grp"), lax.axis_index("dev")
     me = group * n + member
-    partner = member + 1 - 2 * lax.rem(member, 2)
+    place, parity = lax.div(member, 2), lax.rem(member, 2)
+    partner = member + 1 - 2 * parity
     before = lax.rem(group + groups - 1, groups)
     pools = (dens_pool, ortho_pool, fock_pool)
 
@@ -92,40 +93,88 @@
             device_id_type=MESH,
         )
 
-    def ship(m, src, slot, send_slot, device):
-        remote(src, pools[m].at[slot], send.at[m, send_slot], recv.at[m, slot], device).start()
+    RIGHT, LEFT, PARTNER, BEFORE = 0, 1, 2, 3
+
+    def link(way):
+        return (
+            (group, member + 2), (group, member - 2), (group, partner), (before, member)
+        )[way]
+
+    def copy(m, way, slot, src=None):
+        pool = pools[m]
+        target = n + slot if way == BEFORE else slot
+        return remote(
+            pool.at[slot] if src is None else src,
+            pool.at[target],
+            send.at[m, way, slot],
+            recv.at[m, target],
+            link(way),
+        )
 
     def arrived(m, slot):
         pool = pools[m]
         remote(
-            pool.at[slot], pool.at[slot], send.at[m, 0], recv.at[m, slot], (group, partner)
+            pool.at[slot], pool.at[slot], send.at[m, PARTNER, 0], recv.at[m, slot], link(PARTNER)
         ).wait_recv()
 
+    has_right, has_left = place < half - 1, place > 0
+
     def start_own(m, src):
-        for k in range(1, half):
-            ship(m, src, member, k - 1, (group, lax.rem(member + 2 * k, n)))
-        ship(m, src, member, half - 1, (group, partner))
-        ship(m, src, n + member, n - 1, (before, member))
+        pl.when(has_right)(lambda: copy(m, RIGHT, member, src).start())
+        pl.when(has_left)(lambda: copy(m, LEFT, member, src).start())
+        copy(m, PARTNER, member, src).start()
+        copy(m, BEFORE, member, src).start()
+
+    def from_left(k, act):
+        pl.when(place >= k)(lambda: act(2 * (place - k)))
+
+    def from_right(k, act):
+        pl.when(place + k < half)(lambda: act(2 * (place + k)))
+
+    def both_sides(k, left_act, right_act):
+        from_left(k, left_act)
+        from_right(k, right_act)
 
     def take_line(m, k):
-        slot = lax.rem(member + 2 * k, n)
-        arrived(m, slot)
-        ship(m, pools[m].at[slot], slot, half - 1 + k, (group, partner))
-        ship(m, pools[m].at[slot], n + slot, n - 1 + k, (before, member))
-        return slot
+        def pass_on(slot):
+            copy(m, PARTNER, slot).start()
+            copy(m, BEFORE, slot).start()
+
+        def left_act(base):
+            slot = base + parity
+            arrived(m, slot)
+            pl.when(has_right)(lambda: copy(m, RIGHT, slot).start())
+            pass_on(slot)
+
+        def right_act(base):
+            slot = base + parity
+            arrived(m, slot)
+            pl.when(has_left)(lambda: copy(m, LEFT, slot).start())
+            pass_on(slot)
+
+        both_sides(k, left_act, right_act)
 
     def take_partner(m, k):
-        slot = lax.rem(partner + 2 * k, n)
-        arrived(m, slot)
-        ship(m, pools[m].at[slot], n + slot, n - 1 + half + k, (before, member))
-        return slot
+        def act(base):
+            slot = base + (1 - parity)
+            arrived(m, slot)
+            copy(m, BEFORE, slot).start()
+
+        if isinstance(k, int) and k == 0:
+            act(2 * place)
+        else:
+            both_sides(k, act, act)
+
+    def take_partners(m):
+        take_partner(m, 0)
+        loop(1, half, lambda k: take_partner(m, k))
 
     dens_pool[member] = dens[0]
     ortho_pool[member] = ortho[0]
     start_own(0, dens.at[0])
     loop(1, half, lambda k: take_line(0, k))
     start_own(1, ortho.at[0])
-    loop(0, half, lambda k: take_partner(0, k))
+    take_partners(0)
 
     def coefficients(p):
         totals = [jnp.zeros((8, basis), F32) for _ in range(n)]
@@ -147,30 +196,53 @@
             value = value + coef[p, pl.ds(slot, 1), :] * fit[p, at : at + size, :].astype(F32)
         return value
 
-    def send_part(k):
-        slot = lax.rem(member + k, n)
+    def to_partner(line):
+        return remote(
+            part.at[line], inbox.at[line], part_send.at[line], part_recv.at[line], (group, partner)
+        )
+
+    def along(line, arriving):
+        return remote(
+            part.at[half + line],
+            inbox.at[half + arriving],
+            part_send.at[half + line],
+            part_recv.at[half + arriving],
+            (group, 2 * line + parity),
+        )
+
+    def give_partner(k):
+        line = lax.rem(place + k, half)
         for at, size in row_chunks(basis):
-            part[k, at : at + size, :] = partial(slot, at, size).astype(BF)
-        remote(
-            part.at[k], inbox.at[k], part_send.at[k], part_recv.at[k], (group, slot)
-        ).start()
-
-    loop(1, n, send_part)
+            part[line, at : at + size, :] = partial(2 * line + 1 - parity, at, size).astype(BF)
+        to_partner(line).start()
+
+    def give_line(k):
+        line = lax.rem(place + k, half)
+        to_partner(line).wait_recv()
+        for at, size in row_chunks(basis):
+            both = partial(2 * line + parity, at, size) + inbox[line, at : at + size, :].astype(F32)
+            part[half + line, at : at + size, :] = both.astype(BF)
+        along(line, place).start()
+
+    loop(1, half, give_partner)
+    give_partner(0)
+    loop(1, half, give_line)
     for at, size in row_chunks(basis):
         sums[at : at + size, :] = (
             partial(member, at, size)
             + core[0, at : at + size, :].astype(F32)
             + embed[0, at : at + size, :].astype(F32)
         )
-    loop(0, half, lambda k: take_partner(1, k))
+    take_partners(1)
+    to_partner(place).wait_recv()
+    sums[...] += inbox[place].astype(F32)
 
     def add_part(k):
-        remote(
-            part.at[k], inbox.at[k], part_send.at[k], part_recv.at[k], (group, partner)
-        ).wait()
-        sums[...] += inbox[k].astype(F32)
-
-    loop(1, n, add_part)
+        line = lax.rem(place + k, half)
+        along(line, line).wait_recv()
+        sums[...] += inbox[half + line].astype(F32)
+
+    loop(1, half, add_part)
     fock_pool[member] = sums[...].astype(BF)
     start_own(2, fock_pool.at[member])
 
@@ -210,8 +282,19 @@
         value = jnp.sum(jnp.sum(terms, axis=0, keepdims=True), axis=1, keepdims=True)
         table[me] = table[me] + jnp.where(lanes == slot, value + mono, 0.0)
 
-    loop(1, half, lambda k: pair(take_line(2, k)))
-    loop(0, half, lambda k: pair(take_partner(2, k)))
+    def line_pairs(k):
+        take_line(2, k)
+        both_sides(k, lambda base: pair(base + parity), lambda base: pair(base + parity))
+
+    loop(1, half, line_pairs)
+    take_partner(2, 0)
+    pair(partner)
+
+    def partner_pairs(k):
+        take_partner(2, k)
+        both_sides(k, lambda base: pair(base + 1 - parity), lambda base: pair(base + 1 - parity))
+
+    loop(1, half, partner_pairs)
 
     def next_pair(k):
         slot = n + lax.rem(member + k, n)
@@ -234,14 +317,18 @@
     loop(1, total, take_row)
     table_out[...] = table[...]
 
-    def sent(k):
+    def sent(line):
+        slot = 2 * line + parity
+        to_partner(line).wait_send()
+        pl.when(line != place)(lambda: along(line, line).wait_send())
         for m in range(3):
-            pool = pools[m]
-            remote(
-                pool.at[0], pool.at[0], send.at[m, k], recv.at[m, 0], (group, partner)
-            ).wait_send()
-
-    loop(0, 2 * n - 1, sent)
+            pl.when(has_right & (line <= place))(lambda: copy(m, RIGHT, slot).wait_send())
+            pl.when(has_left & (line >= place))(lambda: copy(m, LEFT, slot).wait_send())
+            copy(m, PARTNER, slot).wait_send()
+            copy(m, BEFORE, slot).wait_send()
+            copy(m, BEFORE, 2 * line + 1 - parity).wait_send()
+
+    loop(0, half, sent)
 
 
 def on_device(dens, core, embed, fit, ortho, pairs, assignment, owner_map):
@@ -267,7 +354,7 @@
             pltpu.VMEM((3,) + square, BF),
             pltpu.VMEM(square, F32),
             pltpu.VMEM((total, 1, 128), F32),
-            dma((3, 2 * members - 1)),
+            dma((3, 4, members)),
             dma((3, 2 * members)),
             dma((members,)),
             dma((members,)),

time: 92 us -> 87.4 us (0.950)
  Pallas kernels: 85.1 us -> 80.5 us
    pallas_call x1, Pallas kernels: 85.1 us -> 80.5 us  [on_device(): pl.pallas_call(functools.partial(kernel, members, groups), out_shape=jax....]
where the time goes in v3:
time: 87.4 us; the launch traced here: 87 us
  Pallas kernels  80.5 us (92%)
  other arithmetic  4 us (5%)
  local copies, waits for them, and re-layouts  1.86 us (2%)
    pallas_call x1, Pallas kernels, on_device(): pl.pallas_call(functools.partial(kernel, members, groups), out_shape=jax....  80.5 us

profile of v3, /device:TPU:0, one launch (start us, length us, event | category | flops | bytes accessed | tf_op | source)
XLA Modules:
  0.0 87.0 jit_solution(9526644286926111230)
XLA Ops:
  0.6 0.8 convert_bitcast_fusion
  1.4 0.1 copy.12
  1.5 0.1 reduce-window.9
  1.6 0.1 reduce
  1.8 0.8 slice_reduce_fusion.2
  2.5 0.7 select_reduce_fusion.3
  3.3 80.5 %shard_map.95 = f32[32,1,128]{2,1,0:T(1,128)} custom-call(bf16[1,200,200]{2,1,0:T(8,128)(2,1)} %dens.1, bf16[1,200,200]{2,1,0:T(8,128)(2,1)} %core.1, bf16[1,200,200]{2,1,0:T(8,128)(2,1)} %embed.1, bf16[24,200,200]{2,1,0:T(8,128)(2,1)} %fit.1, bf16[1,200,200]{2,1,0:T(8,128)(2,1)} %ortho.1), custom_call_target="tpu_custom_call" | custom-call | tf_op jit(solution)/shard_map/pallas_call | solution.py:342
  83.8 0.9 select_reduce_fusion
  84.7 0.9 %slice_reduce_fusion = f32[32]{0:T(128)S(1)} fusion(f32[32,128]{1,0:T(8,128)} %bitcast.5), kind=kLoop, calls=%fused_computation.10 | loop fusion | bytes 256 | tf_op jit(solution)/shard_map/slice | solution.py:370
  85.6 0.1 select_reduce_fusion.1
  85.7 0.6 fusion.6
  86.3 0.1 dynamic_slice.7
  86.4 0.6 select_reduce_fusion.5
  (4 shorter events, 0.1 us)

commit v4 on v3

--- a/solution.py
+++ b/solution.py
@@ -119,11 +119,13 @@
 
     has_right, has_left = place < half - 1, place > 0
 
-    def start_own(m, src):
-        pl.when(has_right)(lambda: copy(m, RIGHT, member, src).start())
-        pl.when(has_left)(lambda: copy(m, LEFT, member, src).start())
-        copy(m, PARTNER, member, src).start()
-        copy(m, BEFORE, member, src).start()
+    def start_own(m, src, ways=(RIGHT, LEFT, PARTNER, BEFORE)):
+        if RIGHT in ways:
+            pl.when(has_right)(lambda: copy(m, RIGHT, member, src).start())
+            pl.when(has_left)(lambda: copy(m, LEFT, member, src).start())
+        for way in ways:
+            if way >= PARTNER:
+                copy(m, way, member, src).start()
 
     def from_left(k, act):
         pl.when(place >= k)(lambda: act(2 * (place - k)))
@@ -135,9 +137,10 @@
         from_left(k, left_act)
         from_right(k, right_act)
 
-    def take_line(m, k):
+    def take_line(m, k, partner_too=True):
         def pass_on(slot):
-            copy(m, PARTNER, slot).start()
+            if partner_too:
+                copy(m, PARTNER, slot).start()
             copy(m, BEFORE, slot).start()
 
         def left_act(base):
@@ -173,27 +176,36 @@
     ortho_pool[member] = ortho[0]
     start_own(0, dens.at[0])
     loop(1, half, lambda k: take_line(0, k))
-    start_own(1, ortho.at[0])
+    start_own(1, ortho.at[0], (RIGHT, LEFT, BEFORE))
+
+    def coefficients(side):
+        def step(p):
+            totals = [jnp.zeros((8, basis), F32) for _ in range(half)]
+            for at, size in row_chunks(basis):
+                factor = fit[p, at : at + size, :].astype(F32)
+                for line in range(half):
+                    prod = dens_pool[2 * line + side, at : at + size, :].astype(F32) * factor
+                    totals[line] = totals[line] + jnp.sum(
+                        prod.reshape(size // 8, 8, basis), axis=0
+                    )
+            stacked = jnp.concatenate(
+                [jnp.sum(t, axis=0, keepdims=True) for t in totals], axis=0
+            )
+            value = jnp.sum(stacked, axis=1, keepdims=True).astype(BF).astype(F32)
+            coef[side, p] = jnp.broadcast_to(value, (half, basis))
+
+        loop(0, aux, step)
+
+    coefficients(parity)
+    loop(1, half, lambda k: take_line(1, k, False))
     take_partners(0)
-
-    def coefficients(p):
-        totals = [jnp.zeros((8, basis), F32) for _ in range(n)]
-        for at, size in row_chunks(basis):
-            factor = fit[p, at : at + size, :].astype(F32)
-            for f in range(n):
-                prod = dens_pool[f, at : at + size, :].astype(F32) * factor
-                totals[f] = totals[f] + jnp.sum(prod.reshape(size // 8, 8, basis), axis=0)
-        stacked = jnp.concatenate([jnp.sum(t, axis=0, keepdims=True) for t in totals], axis=0)
-        value = jnp.sum(stacked, axis=1, keepdims=True).astype(BF).astype(F32)
-        coef[p] = jnp.broadcast_to(value, (n, basis))
-
-    loop(0, aux, coefficients)
-    loop(1, half, lambda k: take_line(1, k))
+    coefficients(1 - parity)
 
     def partial(slot, at, size):
+        side, line = lax.rem(slot, 2), lax.div(slot, 2)
         value = jnp.zeros((size, basis), F32)
         for p in range(aux):
-            value = value + coef[p, pl.ds(slot, 1), :] * fit[p, at : at + size, :].astype(F32)
+            value = value + coef[side, p, pl.ds(line, 1), :] * fit[p, at : at + size, :].astype(F32)
         return value
 
     def to_partner(line):
@@ -226,6 +238,13 @@
 
     loop(1, half, give_partner)
     give_partner(0)
+    start_own(1, ortho.at[0], (PARTNER,))
+
+    def ortho_across(k):
+        act = lambda base: copy(1, PARTNER, base + parity).start()
+        both_sides(k, act, act)
+
+    loop(1, half, ortho_across)
     loop(1, half, give_line)
     for at, size in row_chunks(basis):
         sums[at : at + size, :] = (
@@ -348,7 +367,7 @@
             pltpu.VMEM((2 * members,) + square, BF),
             pltpu.VMEM((2 * members,) + square, BF),
             pltpu.VMEM((2 * members,) + square, BF),
-            pltpu.VMEM((aux, members, basis), F32),
+            pltpu.VMEM((2, aux, members // 2, basis), F32),
             pltpu.VMEM((members,) + square, BF),
             pltpu.VMEM((members,) + square, BF),
             pltpu.VMEM((3,) + square, BF),

time: 87.4 us -> 93.3 us (1.068)
  Pallas kernels: 80.5 us -> 86.3 us
    pallas_call x1, Pallas kernels: 80.5 us -> 86.3 us  [on_device(): pl.pallas_call(functools.partial(kernel, members, groups), out_shape=jax....]
where the time goes in v4:
time: 93.3 us; the launch traced here: 92.8 us
  Pallas kernels  86.3 us (92%)
  other arithmetic  4 us (4%)
  local copies, waits for them, and re-layouts  1.86 us (2%)
    pallas_call x1, Pallas kernels, on_device(): pl.pallas_call(functools.partial(kernel, members, groups), out_shape=jax....  86.3 us

profile of v4, /device:TPU:0, one launch (start us, length us, event | category | flops | bytes accessed | tf_op | source)
XLA Modules:
  0.0 92.8 jit_solution(5700998781306028329)
XLA Ops:
  0.6 0.8 convert_bitcast_fusion
  1.4 0.1 copy.12
  1.5 0.1 reduce-window.9
  1.6 0.1 reduce
  1.8 0.8 slice_reduce_fusion.2
  2.5 0.7 select_reduce_fusion.3
  3.3 86.3 %shard_map.95 = f32[32,1,128]{2,1,0:T(1,128)} custom-call(bf16[1,200,200]{2,1,0:T(8,128)(2,1)} %dens.1, bf16[1,200,200]{2,1,0:T(8,128)(2,1)} %core.1, bf16[1,200,200]{2,1,0:T(8,128)(2,1)} %embed.1, bf16[24,200,200]{2,1,0:T(8,128)(2,1)} %fit.1, bf16[1,200,200]{2,1,0:T(8,128)(2,1)} %ortho.1), custom_call_target="tpu_custom_call" | custom-call | tf_op jit(solution)/shard_map/pallas_call | solution.py:361
  89.6 0.9 select_reduce_fusion
  90.5 0.9 slice_reduce_fusion
  91.4 0.1 select_reduce_fusion.1
  91.5 0.6 fusion.6
  92.1 0.1 dynamic_slice.7
  92.2 0.6 select_reduce_fusion.5
  (4 shorter events, 0.1 us)

commit v5 on v4

--- a/solution.py
+++ b/solution.py
@@ -176,7 +176,7 @@
     ortho_pool[member] = ortho[0]
     start_own(0, dens.at[0])
     loop(1, half, lambda k: take_line(0, k))
-    start_own(1, ortho.at[0], (RIGHT, LEFT, BEFORE))
+    start_own(1, ortho.at[0])
 
     def coefficients(side):
         def step(p):
@@ -197,7 +197,7 @@
         loop(0, aux, step)
 
     coefficients(parity)
-    loop(1, half, lambda k: take_line(1, k, False))
+    loop(1, half, lambda k: take_line(1, k))
     take_partners(0)
     coefficients(1 - parity)
 
@@ -238,13 +238,6 @@
 
     loop(1, half, give_partner)
     give_partner(0)
-    start_own(1, ortho.at[0], (PARTNER,))
-
-    def ortho_across(k):
-        act = lambda base: copy(1, PARTNER, base + parity).start()
-        both_sides(k, act, act)
-
-    loop(1, half, ortho_across)
     loop(1, half, give_line)
     for at, size in row_chunks(basis):
         sums[at : at + size, :] = (
@@ -252,7 +245,6 @@
             + core[0, at : at + size, :].astype(F32)
             + embed[0, at : at + size, :].astype(F32)
         )
-    take_partners(1)
     to_partner(place).wait_recv()
     sums[...] += inbox[place].astype(F32)
 
@@ -264,6 +256,7 @@
     loop(1, half, add_part)
     fock_pool[member] = sums[...].astype(BF)
     start_own(2, fock_pool.at[member])
+    take_partners(1)
 
     fock, d, x = fock_pool[member], dens[0], ortho[0]
     v = dot(fock, x).astype(BF)

time: 93.3 us -> 85.3 us (0.914)
  Pallas kernels: 86.3 us -> 78.4 us
    pallas_call x1, Pallas kernels: 86.3 us -> 78.4 us  [on_device(): pl.pallas_call(functools.partial(kernel, members, groups), out_shape=jax....]
where the time goes in v5:
time: 85.3 us; the launch traced here: 84.9 us
  Pallas kernels  78.4 us (92%)
  other arithmetic  4 us (5%)
  local copies, waits for them, and re-layouts  1.86 us (2%)
    pallas_call x1, Pallas kernels, on_device(): pl.pallas_call(functools.partial(kernel, members, groups), out_shape=jax....  78.4 us

profile of v5, /device:TPU:0, one launch (start us, length us, event | category | flops | bytes accessed | tf_op | source)
XLA Modules:
  0.0 84.9 jit_solution(10943616044992608375)
XLA Ops:
  0.6 0.8 convert_bitcast_fusion
  1.4 0.1 copy.12
  1.5 0.1 reduce-window.9
  1.6 0.1 reduce
  1.8 0.8 slice_reduce_fusion.2
  2.5 0.7 select_reduce_fusion.3
  3.3 78.4 %shard_map.95 = f32[32,1,128]{2,1,0:T(1,128)} custom-call(bf16[1,200,200]{2,1,0:T(8,128)(2,1)} %dens.1, bf16[1,200,200]{2,1,0:T(8,128)(2,1)} %core.1, bf16[1,200,200]{2,1,0:T(8,128)(2,1)} %embed.1, bf16[24,200,200]{2,1,0:T(8,128)(2,1)} %fit.1, bf16[1,200,200]{2,1,0:T(8,128)(2,1)} %ortho.1), custom_call_target="tpu_custom_call" | custom-call | tf_op jit(solution)/shard_map/pallas_call | solution.py:354
  81.7 0.9 %select_reduce_fusion = f32[384,16]{0,1:T(8,128)S(1)} fusion(f32[32,16]{1,0:T(8,128)} %bitcast.4, pred[384,32]{0,1:T(8,128)(4,1)S(1)} %iota_compare_fusion.1), kind=kLoop, calls=%fused_computation | loop fusion | flops 387072 | bytes 38912 | tf_op jit(solution)/shard_map/reduce_sum | solution.py:31
  82.6 0.9 %slice_reduce_fusion = f32[32]{0:T(128)S(1)} fusion(f32[32,128]{1,0:T(8,128)} %bitcast.5), kind=kLoop, calls=%fused_computation.10 | loop fusion | bytes 256 | tf_op jit(solution)/shard_map/slice | solution.py:382
  83.5 0.1 select_reduce_fusion.1
  83.6 0.6 fusion.6
  84.2 0.1 dynamic_slice.7
  84.3 0.6 select_reduce_fusion.5
  (4 shorter events, 0.1 us)
